TPU v7x, 128 devices: a whole 4x4x4 slice. The times are simulated.
128 devices in a mesh: seq: 32 (over z, x, core), rep: 4 (over y).
Axes of the slice: x: 4, y: 4, z: 4, core: 2. Of those that a mesh axis runs over, the one named last changes fastest.
Arguments:
- tokens: bfloat16 [16384, 2304], P(('rep', 'seq')), parts along dimension 0, may hold values from -6 to 6
- qkv_weight: bfloat16 [2304, 6144], P(None, 'seq'), may hold values from -0.125 to 0.125
- conv_weight: float32 [4, 6144], replicated, may hold values from -3 to 3
- decay_down: bfloat16 [2304, 128], replicated, may hold values from -0.125 to 0.125
- decay_up: bfloat16 [128, 2048], replicated, may hold values from -0.5 to 0.5
- decay_rate: float32 [2048], replicated, may hold values from 0.00024414062 to 0.1
- beta_weight: bfloat16 [2304, 16], replicated, may hold values from -0.125 to 0.125
- beta_scale: float32 [16], replicated, may hold values from 0.03125 to 1
- gate_down: bfloat16 [2304, 128], replicated, may hold values from -0.125 to 0.125
- gate_up: bfloat16 [128, 2048], replicated, may hold values from -0.5 to 0.5
- norm_gain: float32 [128], replicated, may hold values from 0.1 to 1.9
Outputs:
- attended: bfloat16 [16384, 2048], P(('rep', 'seq')), parts along dimension 0
There are 4 independent parts, one for each index of `rep`. A program takes and returns all parts, laid end to end along the dimension named above; an argument that names none is the same for every part. Nothing has to cross between parts.
All inputs are finite; a program needn't handle non-finite values.
Results may differ from a plain program's by a relative error of at most 0.0054.
Values may be sent and summed in bfloat16 or wider, within the bound.
No kernel may reach another device: no remote copies, remote signals or barrier semaphores. Data moves between devices by JAX's collectives and lax.ppermute only.
A program may use at most 192 MiB of HBM per device.

v0:
```python
import jax
import jax.numpy as jnp
from jax import lax
from jax.sharding import PartitionSpec as P

H = 16
DK = 128
CONV = 4
BLOCK = 64
precise = lax.Precision.HIGHEST


def from_behind(block, axis, distance):
    devices = range(lax.axis_size(axis))
    route = [(i - distance, i) for i in devices if i - distance in devices]
    return lax.ppermute(block, axis, route)


def carried_in(x, axis, combine, identity):
    devices, mine = (lax.axis_size(axis), lax.axis_index(axis))
    everything = jax.tree.map(lambda part: lax.all_gather(part, axis), x)
    start = jax.tree.map(
        lambda part, zero: jnp.broadcast_to(jnp.asarray(zero, part.dtype), part.shape), x, identity
    )

    def lap(k, before):
        reached = k < mine
        new = combine(before, jax.tree.map(lambda part: part[k], everything))
        return jax.tree.map(lambda a, b: jnp.where(reached, a, b), new, before)

    return lax.fori_loop(0, devices, lap, start)


def unit_rows(vector):
    return vector * lax.rsqrt(jnp.sum(vector * vector, axis=-1, keepdims=True) + 1e-06)


def features(padded, count, conv_weight):
    combined = conv_weight[0] * padded[0:count].astype(jnp.float32)
    for offset in range(1, CONV):
        combined = combined + conv_weight[offset] * padded[offset : offset + count].astype(
            jnp.float32
        )
    active = jax.nn.silu(combined).reshape(count, 3, H, DK)
    query = unit_rows(active[:, 0]) * DK ** (-0.5)
    keys = unit_rows(active[:, 1])
    values = active[:, 2]
    return (query, keys, values)


def gates(tokens, decay_down, decay_up, decay_rate, beta_weight, beta_scale, gate_down, gate_up):
    beta = beta_scale * jax.nn.sigmoid(
        jnp.dot(tokens, beta_weight, preferred_element_type=jnp.float32)
    )
    decay_low = jnp.dot(tokens, decay_down, preferred_element_type=jnp.float32).astype(jnp.bfloat16)
    logdec = -decay_rate * jax.nn.sigmoid(
        jnp.dot(decay_low, decay_up, preferred_element_type=jnp.float32)
    )
    gate_low = jnp.dot(tokens, gate_down, preferred_element_type=jnp.float32).astype(jnp.bfloat16)
    gate_value = jax.nn.sigmoid(jnp.dot(gate_low, gate_up, preferred_element_type=jnp.float32))
    return (beta, logdec, gate_value)


def to_blocks(array, count):
    return array.reshape(count // BLOCK, BLOCK, H, array.shape[-1]).transpose(0, 2, 1, 3)


def block_terms(query, keys, values, beta, logdec):
    log_sum = jnp.cumsum(logdec, axis=2)
    grow = jnp.exp(log_sum)
    keys_up = keys * grow
    keys_down = keys * jnp.exp(-log_sum)
    query_up = query * grow
    keys_end = keys * jnp.exp(log_sum[:, :, -1:, :] - log_sum)
    length = query.shape[2]
    rows = lax.broadcasted_iota(jnp.int32, (length, length), 0)
    columns = lax.broadcasted_iota(jnp.int32, (length, length), 1)
    scores = jnp.einsum("nhic,nhjc->nhij", keys_up, keys_down, precision=precise) * beta[..., None]
    system = jnp.where(rows > columns, scores, 0.0) + jnp.eye(length, dtype=jnp.float32)
    right_side = jnp.concatenate([values, keys_up], axis=-1) * beta[..., None]
    solved = jax.scipy.linalg.solve_triangular(system, right_side, lower=True, unit_diagonal=True)
    values_w = solved[..., :DK]
    keys_w = solved[..., DK:]
    attend = jnp.where(
        rows >= columns, jnp.einsum("nhic,nhjc->nhij", query_up, keys_down, precision=precise), 0.0
    )
    decay_end = jnp.exp(log_sum[:, :, -1, :])
    return (query_up, keys_end, values_w, keys_w, attend, decay_end)


def advance(state, inputs):
    query_up, keys_end, values_w, keys_w, attend, decay_end = inputs
    update = values_w - jnp.einsum("hcd,hde->hce", keys_w, state, precision=precise)
    output = jnp.einsum("hcd,hde->hce", query_up, state, precision=precise)
    output = output + jnp.einsum("hij,hje->hie", attend, update, precision=precise)
    state = decay_end[..., None] * state + jnp.einsum(
        "hcd,hce->hde", keys_end, update, precision=precise
    )
    return (state, output)


def matmul(left, right):
    return jnp.einsum("...de,...ef->...df", left, right, precision=precise)


def fold_block(carry, inputs):
    matrix, offset = carry
    keys_end, keys_w, values_w, decay_end = inputs
    eye_block = jnp.eye(DK, dtype=jnp.float32)
    block_matrix = decay_end[..., None] * eye_block - jnp.einsum(
        "hcd,hce->hde", keys_end, keys_w, precision=precise
    )
    block_offset = jnp.einsum("hcd,hce->hde", keys_end, values_w, precision=precise)
    return ((matmul(block_matrix, matrix), matmul(block_matrix, offset) + block_offset), None)


def join_pairs(first, second):
    return (matmul(second[0], first[0]), matmul(second[0], first[1]) + second[1])


def finish(core, gate_value, norm_gain, count):
    scaled = core * lax.rsqrt(jnp.mean(core * core, axis=-1, keepdims=True) + 1e-06) * norm_gain
    return (scaled.reshape(count, H * DK) * gate_value).astype(jnp.bfloat16)


def per_device(
    tokens,
    qkv_weight,
    conv_weight,
    decay_down,
    decay_up,
    decay_rate,
    beta_weight,
    beta_scale,
    gate_down,
    gate_up,
    norm_gain,
):
    count = tokens.shape[0]
    mixed = jnp.dot(
        tokens,
        lax.all_gather(qkv_weight, "seq", axis=1, tiled=True),
        preferred_element_type=jnp.float32,
    ).astype(jnp.bfloat16)
    earlier = from_behind(mixed[count - (CONV - 1) :], "seq", 1)
    padded = jnp.concatenate([earlier, mixed], axis=0)
    query, keys, values = features(padded, count, conv_weight)
    beta, logdec, gate_value = gates(
        tokens, decay_down, decay_up, decay_rate, beta_weight, beta_scale, gate_down, gate_up
    )
    beta_blocks = beta.reshape(count // BLOCK, BLOCK, H).transpose(0, 2, 1)
    terms = block_terms(
        to_blocks(query, count),
        to_blocks(keys, count),
        to_blocks(values, count),
        beta_blocks,
        to_blocks(logdec.reshape(count, H, DK), count),
    )
    query_up, keys_end, values_w, keys_w, attend, decay_end = terms
    identity = jnp.broadcast_to(jnp.eye(DK, dtype=jnp.float32), (H, DK, DK))
    zeroed = jnp.zeros((H, DK, DK), jnp.float32)
    (matrix, offset), unused = lax.scan(
        fold_block, (identity, zeroed), (keys_end, keys_w, values_w, decay_end)
    )

    def combine(earlier_pair, later_pair):
        return join_pairs(earlier_pair, later_pair)

    prefix = carried_in((matrix, offset), "seq", combine, (identity, zeroed))
    incoming = prefix[1]
    final_state, outputs = lax.scan(advance, incoming, terms)
    core = outputs.transpose(0, 2, 1, 3).reshape(count, H, DK)
    return finish(core, gate_value, norm_gain, count)


def solution(mesh):
    in_specs = (
        P(("rep", "seq"), None),
        P(None, "seq"),
        P(),
        P(),
        P(),
        P(),
        P(),
        P(),
        P(),
        P(),
        P(),
    )
    out_specs = P(("rep", "seq"), None)
    return jax.shard_map(
        per_device, mesh=mesh, in_specs=in_specs, out_specs=out_specs, check_vma=False
    )
```

profile of v0, /device:TPU:1, one launch (start us, length us, event | category | flops | bytes accessed | tf_op | source)
XLA Modules:
  0.0 684.3 jit_solution(2664302093057689382)
XLA Ops:
  10.9 13.1 %fusion.63 = f32[2,16,64,128]{3,1,2,0:T(8,128)S(1)} fusion(f32[2,64,16,128]{3,2,1,0:T(8,128)S(1)} %bitcast.180), kind=kOutput, calls=%fused_computation.87 | output fusion | flops 16515072 | bytes 2097152 | tf_op jit(solution)/shard_map/jit(cumsum)/reduce_window_sum | solution.py:69
  24.4 89.2 %all-gather.6.cloned.1.call-done = bf16[2304,6144]{0,1:T(8,128)(2,1)} async-done(((bf16[2304,192]{0,1:T(8,128)(2,1)}), bf16[2304,6144]{0,1:T(8,128)(2,1)}) %all-gather.6.cloned.1.call-update) | async-done | bytes 28311568 | tf_op jit(solution)/shard_map/all_gather | solution.py:142
  113.6 14.3 %convolution_convert_fusion = bf16[128,6144]{1,0:T(8,128)(2,1)S(1)} fusion(bf16[128,2304]{1,0:T(8,128)(2,1)S(1)} %copy-done, bf16[2304,6144]{0,1:T(8,128)(2,1)} %all-gather.6.cloned.1.call-done), kind=kOutput, calls=%fused_computation.48 | convolution fusion | flops 3624665088 | bytes 30474240 | tf_op jit(solution)/shard_map/dot_general | solution.py:140
  128.6 3.4 collective-permute-start
  139.4 3.3 fusion.57
  142.7 158.7 %custom-call.4 = f32[2,16,1,64,64]{3,4,2,1,0:T(8,128)} custom-call(f32[2,16,1,64,64]{4,3,2,1,0:T(8,128)} %fusion.57), custom_call_target="InvertDiagBlocksLowerTriangular" | custom-call | tf_op jit(solution)/shard_map/jit(_solve_triangular)/vmap(vmap())/triangular_solve | solution.py:81
  303.0 3.0 fusion.48
  309.2 20.1 %while.40 = (s32[]{:T(128)}, f32[16,128,128]{2,1,0:T(8,128)}, f32[16,128,128]{2,1,0:T(8,128)}, f32[2,16,128]{2,1,0:T(8,128)S(1)}, f32[2,16,64,128]{3,2,1,0:T(8,1...) while((s32[]{:T(128)}, f32[16,128,128]{2,1,0:T(8,128)}, ...), condition=%wide.region_3.4_spmd.clone, body=%wide.region_2.3_spmd.clone.sunk | while | flops 1209040896 | bytes 22177956 | solution.py:162
  309.2 3.1 convolution_subtract_fusion.5
  318.6 3.1 convolution_subtract_fusion.5
  332.7 4.8 convolution_select_fusion
  337.5 107.0 %all-gather.8.cloned.1.call-done = f32[512,128,128]{2,1,0:T(8,128)} async-done(((f32[16,128,128]{2,1,0:T(8,128)}), f32[512,128,128]{2,1,0:T(8,128)}) %all-gather.8.cloned.1.call-update) | async-done | bytes 33554448 | tf_op jit(solution)/shard_map/all_gather | solution.py:21
  444.5 115.5 %all-gather.10.cloned.1.call-done = f32[512,128,128]{2,1,0:T(8,128)} async-done(((f32[16,128,128]{2,1,0:T(8,128)}), f32[512,128,128]{2,1,0:T(8,128)}) %all-gather.10.cloned.1.call-update) | async-done | bytes 33554448 | tf_op jit(solution)/shard_map/all_gather | solution.py:21
  559.9 94.0 %while.41 = (s32[]{:T(128)}, f32[16,128,128]{2,1,0:T(8,128)S(1)}, s32[]{:T(128)}, f32[32,16,128,128]{3,2,1,0:T(8,128)}, f32[32,16,128,128]{3,2,1,0:T(8,128)}, /*index=5*/s32[]{:T(128)}, s32[]{:T(128)}) while((s32[]{:T(128)}, f32[16,128,128]{2,1,0:T(8,128)S(1)}, s32[]{:T(128)}, f32[32,16,128,128]{3,2,1,0:T(8,128)}, ...), condition=%wide.region_5.6_spmd.clone, body=%wide.region_4.5_spmd.clone.sunk | while | flops 403701760 | bytes 7342687 | solution.py:31
  560.0 2.8 fusion.141
  563.0 2.8 fusion.141
  565.9 2.8 fusion.141
  571.8 2.8 fusion.141
  574.7 2.8 fusion.141
  577.6 2.8 fusion.141
  580.6 2.8 fusion.141
  583.5 2.8 fusion.141
  586.5 2.8 fusion.141
  589.4 2.8 fusion.141
  592.3 2.8 fusion.141
  595.3 2.8 fusion.141
  598.2 2.8 fusion.141
  601.1 2.8 fusion.141
  604.1 2.8 fusion.141
  607.0 2.8 fusion.141
  653.9 17.0 %while.39 = (s32[]{:T(128)}, f32[16,128,128]{2,1,0:T(8,128)S(1)}, f32[2,16,64,128]{3,2,1,0:T(8,128)}, f32[2,16,128]{2,1,0:T(8,128)S(1)}, f32[2,16,64,128]{3,2,1,...) while((s32[]{:T(128)}, f32[16,128,128]{2,1,0:T(8,128)S(1)}, ...), condition=%wide.region_8.9_spmd, body=%wide.region_7.8_spmd.sunk | while | flops 705429504 | bytes 22571712 | solution.py:171
  674.9 2.9 fusion.47
  (158 shorter events, 103.0 us)
Async XLA Ops:
  6.5 1.5 copy-start
  6.5 107.1 %all-gather.6.cloned.1.call-start = ((), (), s32[]{:S(2)}) async-start(), calls=%async_computation | async-start | bytes 29196288 | tf_op jit(solution)/shard_map/all_gather | solution.py:142
  7.3 437.2 %all-gather.8.cloned.1.call-start = ((), (), s32[]{:S(2)}) async-start(), calls=%async_computation.1 | async-start | bytes 34603008 | tf_op jit(solution)/shard_map/all_gather | solution.py:21
  9.9 14.0 %copy-start.12 = (bf16[2304,16]{0,1:T(8,128)(2,1)S(1)}, bf16[2304,16]{0,1:T(8,128)(2,1)}, u32[]{:S(2)}) copy-start(bf16[2304,16]{0,1:T(8,128)(2,1)} %param.23) | copy-start | bytes 221188
  9.9 14.0 %copy-start.15 = (f32[16]{0:T(128)S(1)}, f32[16]{0:T(128)}, u32[]{:S(2)}) copy-start(f32[16]{0:T(128)} %param.24) | copy-start | bytes 196
  10.0 14.3 %copy-start.11 = (f32[4,6144]{1,0:T(4,128)S(1)}, f32[4,6144]{1,0:T(4,128)}, u32[]{:S(2)}) copy-start(f32[4,6144]{1,0:T(4,128)} %param.19) | copy-start | bytes 294916
  23.9 104.0 %copy-start.5 = (f32[2,16,64,128]{3,1,2,0:T(8,128)}, f32[2,16,64,128]{3,1,2,0:T(8,128)S(1)}, u32[]{:S(2)}) copy-start(f32[2,16,64,128]{3,1,2,0:T(8,128)S(1)} %fusion.63) | copy-start | bytes 3145732
  128.6 4.7 collective-permute-start
  136.0 1.6 copy-start.6
  137.6 1.8 copy-start.13
  137.6 1.8 copy-start.14
  139.4 163.6 %copy-start.4 = (f32[2,16,64,128]{3,1,2,0:T(8,128)}, f32[2,16,64,128]{3,1,2,0:T(8,128)S(1)}, u32[]{:S(2)}) copy-start(f32[2,16,64,128]{3,1,2,0:T(8,128)S(1)} %get-tuple-element.325) | copy-start | bytes 3145732
  301.4 1.7 copy-start.10
  306.1 1.7 copy-start.7
  309.2 20.9 %copy-start.16 = (f32[128]{0:T(128)S(1)}, f32[128]{0:T(128)}, u32[]{:S(2)}) copy-start(f32[128]{0:T(128)} %param.27) | copy-start | bytes 1540
  312.2 1.2 copy-start.2
  312.3 4.0 copy-start.1
  321.6 2.6 copy-start.2
  321.6 5.4 copy-start.1
  329.3 230.6 %all-gather.10.cloned.1.call-start = ((), (), s32[]{:S(2)}) async-start(), calls=%async_computation.2 | async-start | bytes 34603008 | tf_op jit(solution)/shard_map/all_gather | solution.py:21
  653.9 4.1 copy-start.3
  653.9 4.1 copy-start.8
  659.1 1.0 copy-start.9
  662.4 4.1 copy-start.3
  662.4 4.1 copy-start.8
  667.7 1.0 copy-start.9
  671.0 3.9 copy-start.17
Sparse Core Ops, SparseCore 0:
  9.6 103.9 all-gather.5
  329.4 114.9 all-gather.7
  446.7 113.1 all-gather.9
where the time goes:
time: 686 us; the launch traced here: 684 us
  waiting for transfers between devices  314 us (46%)
  other arithmetic  182 us (27%)
  matrix products  155 us (23%)
  local copies, waits for them, and re-layouts  14.4 us (2%)
  between operations  13.5 us (2%)
    all_gather x2, waiting for transfers between devices, carried_in(): everything = jax.tree.map(lambda part: lax.all_gather(part, axis), x)  222 us
    another operation x2, other arithmetic, block_terms(): jax.scipy.linalg.solve_triangular(system, right_side, lower=True, unit_di...  159 us
    dot_general x36, matrix products, matmul(): return jnp.einsum('...de,...ef->...df', left, right, precision=precise)  98.3 us
    all_gather x1, waiting for transfers between devices, per_device(): lax.all_gather(qkv_weight, 'seq', axis=1, tiled=True)  89.2 us
    dot_general x1, matrix products, per_device(): jnp.dot(tokens, lax.all_gather(qkv_weight, 'seq', axis=1, tiled=True), pr...  14.3 us
  transfers between devices with their start and end apart: 4, of which 4 were waited for; matrix products, arithmetic and copies ran while one was open for 4% of the time, Pallas kernels for 0%

commit v1 on v0

--- a/solution.py
+++ b/solution.py
@@ -139,7 +139,9 @@
     count = tokens.shape[0]
     mixed = jnp.dot(
         tokens,
-        lax.all_gather(qkv_weight, "seq", axis=1, tiled=True),
+        jnp.concatenate(
+            lax.all_to_all(jnp.stack([qkv_weight] * lax.axis_size("seq")), "seq", 0, 0), axis=1
+        ),
         preferred_element_type=jnp.float32,
     ).astype(jnp.bfloat16)
     earlier = from_behind(mixed[count - (CONV - 1) :], "seq", 1)

time: 686 us -> 966 us (1.41)
  waiting for transfers between devices: 314 us -> 571 us
  starting transfers between devices: 3.45 us -> 17.7 us
  local copies, waits for them, and re-layouts: 14.4 us -> 24.8 us
    all_to_all x0 -> x1, waiting for transfers between devices: none -> 333 us  [per_device(): lax.all_to_all(jnp.stack([qkv_weight] * lax.axis_size('seq')), 'seq', 0, 0)]
    all_gather x1 -> x0, waiting for transfers between devices: 89.2 us -> none  [per_device(): lax.all_gather(qkv_weight, 'seq', axis=1, tiled=True)]
    ppermute x1, waiting for transfers between devices: 1.1 us -> 13.3 us  [from_behind(): return lax.ppermute(block, axis, route)]
    another operation x0 -> x1, local copies, waits for them, and re-layouts: none -> 10.4 us  [per_device(): jnp.stack([qkv_weight] * lax.axis_size('seq'))]
  transfers between devices with their start and end apart: 4 -> 4, of which waited for: 4 -> 4; matrix products, arithmetic and copies ran while one was open for 4% -> 2% of each run, Pallas kernels for 0% -> 0%
where the time goes in v1:
time: 966 us; the launch traced here: 964 us
  waiting for transfers between devices  571 us (59%)
  other arithmetic  181 us (19%)
  matrix products  154 us (16%)
  local copies, waits for them, and re-layouts  24.8 us (3%)
  starting transfers between devices  17.7 us (2%)
  between operations  13.8 us (1%)
    all_to_all x1, waiting for transfers between devices, per_device(): lax.all_to_all(jnp.stack([qkv_weight] * lax.axis_size('seq')), 'seq', 0, 0)  333 us
    all_gather x2, waiting for transfers between devices, carried_in(): everything = jax.tree.map(lambda part: lax.all_gather(part, axis), x)  224 us
    another operation x2, other arithmetic, block_terms(): jax.scipy.linalg.solve_triangular(system, right_side, lower=True, unit_di...  159 us
    dot_general x36, matrix products, matmul(): return jnp.einsum('...de,...ef->...df', left, right, precision=precise)  98.3 us
  transfers between devices with their start and end apart: 4, of which 4 were waited for; matrix products, arithmetic and copies ran while one was open for 2% of the time, Pallas kernels for 0%

profile of v1, /device:TPU:1, one launch (start us, length us, event | category | flops | bytes accessed | tf_op | source)
XLA Modules:
  0.0 964.0 jit_solution(10977535629629678419)
XLA Ops:
  6.5 10.4 %stack.2 = bf16[32,2304,192]{1,2,0:T(8,128)(2,1)} broadcast(bf16[2304,192]{0,1:T(8,128)(2,1)} %param.18), dimensions={1,2} | broadcast | bytes 29196288 | tf_op jit(solution)/shard_map/stack | solution.py:143
  17.0 9.6 all-to-all-start
  28.4 13.1 %fusion.63 = f32[2,16,64,128]{3,1,2,0:T(8,128)S(1)} fusion(f32[2,64,16,128]{3,2,1,0:T(8,128)S(1)} %bitcast.183), kind=kOutput, calls=%fused_computation.87 | output fusion | flops 16515072 | bytes 2097152 | tf_op jit(solution)/shard_map/jit(cumsum)/reduce_window_sum | solution.py:69
  41.9 333.0 %all-to-all-done = bf16[32,2304,192]{1,2,0:T(8,128)(2,1)} async-done(((bf16[32,2304,192]{1,2,0:T(8,128)(2,1)}), bf16[32,2304,192]{1,2,0:T(8,128)(2,1)}, u32[]{:S(2)}, u32[]{:S(2)}) %all-to-all-start) | async-done | bytes 28311584 | tf_op jit(solution)/shard_map/all_to_all | solution.py:143
  374.9 14.3 %convolution_convert_fusion = bf16[128,6144]{1,0:T(8,128)(2,1)S(1)} fusion(bf16[128,2304]{1,0:T(8,128)(2,1)S(1)} %copy-done, bf16[2304,6144]{0,1:T(8,128)(2,1)} %bitcast.11), kind=kOutput, calls=%fused_computation.48 | convolution fusion | flops 3624665088 | bytes 30474240 | tf_op jit(solution)/shard_map/dot_general | solution.py:140
  389.9 8.0 collective-permute-start
  398.1 13.3 %collective-permute-done = bf16[3,6144]{1,0:T(4,128)(2,1)S(1)} collective-permute-done((bf16[3,6144]{1,0:T(4,128)(2,1)}, bf16[3,6144]{1,0:T(4,128)(2,1)S(1)}, u32[]{:S(2)}, u32[]{:S(2)}) %collective-permute-start) | collective-permute-done | bytes 36896 | tf_op jit(solution)/shard_map/ppermute | solution.py:16
  417.4 3.3 fusion.57
  420.7 158.7 %custom-call.4 = f32[2,16,1,64,64]{3,4,2,1,0:T(8,128)} custom-call(f32[2,16,1,64,64]{4,3,2,1,0:T(8,128)} %fusion.57), custom_call_target="InvertDiagBlocksLowerTriangular" | custom-call | tf_op jit(solution)/shard_map/jit(_solve_triangular)/vmap(vmap())/triangular_solve | solution.py:81
  581.1 3.0 fusion.48
  587.2 20.1 %while.40 = (s32[]{:T(128)}, f32[16,128,128]{2,1,0:T(8,128)}, f32[16,128,128]{2,1,0:T(8,128)}, f32[2,16,128]{2,1,0:T(8,128)S(1)}, f32[2,16,64,128]{3,2,1,0:T(8,1...) while((s32[]{:T(128)}, f32[16,128,128]{2,1,0:T(8,128)}, ...), condition=%wide.region_3.4_spmd.clone, body=%wide.region_2.3_spmd.clone.sunk | while | flops 1209040896 | bytes 22177956 | solution.py:164
  587.2 3.1 convolution_subtract_fusion.5
  596.6 3.1 convolution_subtract_fusion.5
  610.7 4.8 convolution_select_fusion
  615.5 108.3 %all-gather.5.cloned.1.call-done = f32[512,128,128]{2,1,0:T(8,128)} async-done(((f32[16,128,128]{2,1,0:T(8,128)}), f32[512,128,128]{2,1,0:T(8,128)}) %all-gather.5.cloned.1.call-update) | async-done | bytes 33554448 | tf_op jit(solution)/shard_map/all_gather | solution.py:21
  723.8 115.5 %all-gather.7.cloned.1.call-done = f32[512,128,128]{2,1,0:T(8,128)} async-done(((f32[16,128,128]{2,1,0:T(8,128)}), f32[512,128,128]{2,1,0:T(8,128)}) %all-gather.7.cloned.1.call-update) | async-done | bytes 33554448 | tf_op jit(solution)/shard_map/all_gather | solution.py:21
  839.3 94.0 %while.41 = (s32[]{:T(128)}, f32[16,128,128]{2,1,0:T(8,128)S(1)}, s32[]{:T(128)}, f32[32,16,128,128]{3,2,1,0:T(8,128)}, f32[32,16,128,128]{3,2,1,0:T(8,128)}, /*index=5*/s32[]{:T(128)}, s32[]{:T(128)}) while((s32[]{:T(128)}, f32[16,128,128]{2,1,0:T(8,128)S(1)}, s32[]{:T(128)}, f32[32,16,128,128]{3,2,1,0:T(8,128)}, ...), condition=%wide.region_5.6_spmd.clone, body=%wide.region_4.5_spmd.clone.sunk | while | flops 403701760 | bytes 7342687 | solution.py:31
  839.4 2.8 fusion.141
  842.3 2.8 fusion.141
  845.2 2.8 fusion.141
  848.2 2.8 fusion.141
  851.1 2.8 fusion.141
  854.1 2.8 fusion.141
  857.0 2.8 fusion.141
  859.9 2.8 fusion.141
  862.9 2.8 fusion.141
  865.8 2.8 fusion.141
  868.7 2.8 fusion.141
  871.7 2.8 fusion.141
  874.6 2.8 fusion.141
  933.2 17.1 %while.39 = (s32[]{:T(128)}, f32[16,128,128]{2,1,0:T(8,128)S(1)}, f32[2,16,64,128]{3,2,1,0:T(8,128)}, f32[2,16,128]{2,1,0:T(8,128)S(1)}, f32[2,16,64,128]{3,2,1,...) while((s32[]{:T(128)}, f32[16,128,128]{2,1,0:T(8,128)S(1)}, ...), condition=%wide.region_8.9_spmd, body=%wide.region_7.8_spmd.sunk | while | flops 705429504 | bytes 22571712 | solution.py:173
  954.2 2.9 fusion.47
  (164 shorter events, 107.7 us)
Async XLA Ops:
  6.5 20.1 %copy-start = (bf16[128,2304]{1,0:T(8,128)(2,1)S(1)}, bf16[128,2304]{1,0:T(8,128)(2,1)}, u32[]{:S(2)}) copy-start(bf16[128,2304]{1,0:T(8,128)(2,1)} %param.17) | copy-start | bytes 1769476
  17.0 9.7 %copy-start.15 = (f32[2048]{0:T(1024)S(1)}, f32[2048]{0:T(1024)}, u32[]{:S(2)}) copy-start(f32[2048]{0:T(1024)} %param.22) | copy-start | bytes 24580
  17.0 9.7 %copy-start.18 = (bf16[2304,128]{1,0:T(8,128)(2,1)S(1)}, bf16[2304,128]{1,0:T(8,128)(2,1)}, u32[]{:S(2)}) copy-start(bf16[2304,128]{1,0:T(8,128)(2,1)} %param.20) | copy-start | bytes 1769476
  17.0 9.7 %copy-start.20 = (bf16[128,2048]{1,0:T(8,128)(2,1)S(1)}, bf16[128,2048]{1,0:T(8,128)(2,1)}, u32[]{:S(2)}) copy-start(bf16[128,2048]{1,0:T(8,128)(2,1)} %param.21) | copy-start | bytes 1572868
  17.0 357.9 %all-to-all-start = ((bf16[32,2304,192]{1,2,0:T(8,128)(2,1)}), bf16[32,2304,192]{1,2,0:T(8,128)(2,1)}, u32[]{:S(2)}, u32[]{:S(2)}) async-start(bf16[32,2304,192]{1,2,0:T(8,128)(2,1)} %stack.2), calls=%async_computation | async-start | bytes 56623104 | tf_op jit(solution)/shard_map/all_to_all | solution.py:143
  26.6 697.2 %all-gather.5.cloned.1.call-start = ((), (), s32[]{:S(2)}) async-start(), calls=%async_computation.1 | async-start | bytes 34603008 | tf_op jit(solution)/shard_map/all_gather | solution.py:21
  27.4 14.0 %copy-start.12 = (bf16[2304,16]{0,1:T(8,128)(2,1)S(1)}, bf16[2304,16]{0,1:T(8,128)(2,1)}, u32[]{:S(2)}) copy-start(bf16[2304,16]{0,1:T(8,128)(2,1)} %param.23) | copy-start | bytes 221188
  27.4 14.0 %copy-start.16 = (f32[16]{0:T(128)S(1)}, f32[16]{0:T(128)}, u32[]{:S(2)}) copy-start(f32[16]{0:T(128)} %param.24) | copy-start | bytes 196
  27.5 14.3 %copy-start.11 = (f32[4,6144]{1,0:T(4,128)S(1)}, f32[4,6144]{1,0:T(4,128)}, u32[]{:S(2)}) copy-start(f32[4,6144]{1,0:T(4,128)} %param.19) | copy-start | bytes 294916
  41.4 347.8 %copy-start.5 = (f32[2,16,64,128]{3,1,2,0:T(8,128)}, f32[2,16,64,128]{3,1,2,0:T(8,128)S(1)}, u32[]{:S(2)}) copy-start(f32[2,16,64,128]{3,1,2,0:T(8,128)S(1)} %fusion.63) | copy-start | bytes 3145732
  389.9 21.4 %collective-permute-start = (bf16[3,6144]{1,0:T(4,128)(2,1)}, bf16[3,6144]{1,0:T(4,128)(2,1)S(1)}, u32[]{:S(2)}, u32[]{:S(2)}) collective-permute-start(bf16[3,6144]{1,0:T(4,128)(2,1)} %slice.64), channel_id=1, source_target_pairs={{0,4},{4,8},{8,12},{12,16},{16,20},{20,24},{24,28},{28,32},{32,36}... | collective-permute-start | bytes 110600 | tf_op jit(solution)/shard_map/ppermute | solution.py:16
  414.0 1.6 copy-start.6
  415.7 1.8 copy-start.13
  415.7 1.8 copy-start.14
  417.4 163.6 %copy-start.4 = (f32[2,16,64,128]{3,1,2,0:T(8,128)}, f32[2,16,64,128]{3,1,2,0:T(8,128)S(1)}, u32[]{:S(2)}) copy-start(f32[2,16,64,128]{3,1,2,0:T(8,128)S(1)} %get-tuple-element.341) | copy-start | bytes 3145732
  579.4 1.7 copy-start.10
  584.1 1.6 copy-start.7
  587.2 20.9 %copy-start.17 = (f32[128]{0:T(128)S(1)}, f32[128]{0:T(128)}, u32[]{:S(2)}) copy-start(f32[128]{0:T(128)} %param.27) | copy-start | bytes 1540
  590.3 1.2 copy-start.2
  590.3 4.0 copy-start.1
  599.6 2.6 copy-start.2
  599.7 5.4 copy-start.1
  607.3 232.0 %all-gather.7.cloned.1.call-start = ((), (), s32[]{:S(2)}) async-start(), calls=%async_computation.2 | async-start | bytes 34603008 | tf_op jit(solution)/shard_map/all_gather | solution.py:21
  933.3 4.1 copy-start.3
  933.3 4.1 copy-start.8
  938.5 1.0 copy-start.9
  941.8 4.1 copy-start.3
  941.8 4.1 copy-start.8
  947.0 1.0 copy-start.9
  950.3 3.9 copy-start.19
Sparse Core Ops, SparseCore 0:
  607.4 116.3 all-gather.4
  726.1 113.1 all-gather.6
